TPU v7x, 32 devices: a whole 2x2x4 slice. The times are simulated.
32 devices in a mesh: cell: 2 (over x), blk: 16 (over z, y, core).
Axes of the slice: x: 2, y: 2, z: 4, core: 2. Of those that a mesh axis runs over, the one named last changes fastest.
Arguments:
- psi_val: float32 [256, 64, 64, 64], P('cell', 'blk'), parts along dimension 0, may hold values from -6 to 6
- psi_cond: float32 [6, 64, 64, 64], P('cell', 'blk'), parts along dimension 0, may hold values from -6 to 6
- e_val: float32 [256], P('cell'), parts along dimension 0, may hold values from -8 to -1
- e_cond: float32 [6], P('cell'), parts along dimension 0, may hold values from 1 to 8
- occ: int32 [256], P('cell'), parts along dimension 0, may hold values from 1 to 2
- freq: float32 [10], P('cell'), parts along dimension 0, may hold values from 0.5 to 16
- gmap: int32 [8192], P('cell'), parts along dimension 0, may hold values from 0 to 262143, as said below
Outputs:
- chi_real: float32 [10, 4096, 4096], P('cell', 'blk'), parts along dimension 0
- chi_imag: float32 [10, 4096, 4096], P('cell', 'blk'), parts along dimension 0
There are 2 independent parts, one for each index of `cell`. A program takes and returns all parts, laid end to end along the dimension named above; each array names one. Nothing has to cross between parts.
Inputs may be any that keep to these rules, and one draw needn't show every extreme that they name: `gmap`: the 4096 indices are distinct; index 0 and index 262143 are always among them.
All inputs are finite; a program needn't handle non-finite values.
Results may differ from a plain program's by a relative error of at most 0.0001.
Values sent between devices are 32-bit elements; how exact they have to be, the bound alone decides.
No kernel may reach another device: no remote copies, remote signals or barrier semaphores. Data moves between devices by JAX's collectives and lax.ppermute only.
A program may use at most 256 MiB of HBM per device.

v0:
```python
import math
import jax
import jax.numpy as jnp
from jax import lax
from jax.sharding import PartitionSpec as P

highest = lax.Precision.HIGHEST


def dft_tables(length):
    counter = jnp.arange(length, dtype=jnp.int32)
    angles = (counter[:, None] * counter[None, :] % length).astype(jnp.float32) * (
        2.0 * math.pi / length
    )
    return (jnp.cos(angles), jnp.sin(angles))


def plane_picks(val_part, cond_part, column_idx):
    num_val, planes, size_y, size_z = val_part.shape
    num_cond = cond_part.shape[0]
    pair_count = num_val * num_cond
    density = (val_part[:, None] * cond_part[None]).reshape(pair_count, planes, size_y, size_z)
    cos_z, sin_z = dft_tables(size_z)
    real_a = jnp.einsum("pxyz,zk->ykxp", density, cos_z, precision=highest)
    imag_a = -jnp.einsum("pxyz,zk->ykxp", density, sin_z, precision=highest)
    cos_y, sin_y = dft_tables(size_y)
    real_b = jnp.einsum("ly,ykxp->lkxp", cos_y, real_a, precision=highest) + jnp.einsum(
        "ly,ykxp->lkxp", sin_y, imag_a, precision=highest
    )
    imag_b = jnp.einsum("ly,ykxp->lkxp", cos_y, imag_a, precision=highest) - jnp.einsum(
        "ly,ykxp->lkxp", sin_y, real_a, precision=highest
    )
    return jnp.concatenate(
        [
            jnp.take(real_b.reshape(size_y * size_z, planes, pair_count), column_idx, axis=0),
            jnp.take(imag_b.reshape(size_y * size_z, planes, pair_count), column_idx, axis=0),
        ],
        axis=2,
    )


def phase_sum(values, freq_x, positions, size_x, norm_factor):
    half = values.shape[2] // 2
    angles = (freq_x[:, None] * positions[None, :] % size_x).astype(jnp.float32) * (
        2.0 * math.pi / size_x
    )
    cosine = jnp.cos(angles)[:, :, None]
    sine = jnp.sin(angles)[:, :, None]
    real_v = values[:, :, :half]
    imag_v = values[:, :, half:]
    real_m = jnp.sum(real_v * cosine + imag_v * sine, axis=1)
    imag_m = jnp.sum(imag_v * cosine - real_v * sine, axis=1)
    return jnp.concatenate([real_m, imag_m], axis=1) * norm_factor


def body(psi_val, psi_cond, e_val, e_cond, occ, freq, gmap):
    num_val, planes, size_y, size_z = psi_val.shape
    num_cond = psi_cond.shape[0]
    pairs = num_val * num_cond
    devices_blk = lax.axis_size("blk")
    size_x = planes * devices_blk
    total_points = size_x * size_y * size_z
    norm_factor = 1.0 / math.sqrt(total_points)
    column_idx = gmap % (size_y * size_z)
    plane_freq = gmap // (size_y * size_z)
    picked = plane_picks(psi_val, psi_cond, column_idx)
    positions = lax.axis_index("blk") * planes + jnp.arange(planes, dtype=jnp.int32)
    owned = lax.psum_scatter(
        phase_sum(picked, plane_freq, positions, size_x, norm_factor),
        "blk",
        scatter_dimension=0,
        tiled=True,
    )
    gaps = e_val[:, None] - e_cond[None, :]
    occ_col = occ.astype(jnp.float32)[:, None, None]
    weights = (
        occ_col
        * gaps[:, :, None]
        / (gaps[:, :, None] * gaps[:, :, None] + (freq * freq)[None, None, :])
    )
    weights = weights.reshape(pairs, freq.shape[0]) / math.sqrt(pairs)
    freq_weights = jnp.transpose(weights)[:, None, :]
    real_w = owned[None, :, :pairs] * freq_weights
    imag_w = owned[None, :, pairs:] * freq_weights
    left_side = jnp.stack(
        [jnp.concatenate([real_w, imag_w], axis=2), jnp.concatenate([imag_w, -real_w], axis=2)],
        axis=0,
    )
    chi_both = jnp.einsum(
        "awgk,hk->awgh",
        left_side,
        lax.all_gather(owned, "blk", axis=0, tiled=True),
        precision=highest,
    )
    return (chi_both[0], chi_both[1])


def solution(mesh):
    return jax.shard_map(
        body,
        mesh=mesh,
        in_specs=(
            P("cell", "blk", None, None),
            P("cell", "blk", None, None),
            P("cell"),
            P("cell"),
            P("cell"),
            P("cell"),
            P("cell"),
        ),
        out_specs=(P("cell", "blk", None), P("cell", "blk", None)),
        check_vma=False,
    )
```

profile of v0, /device:TPU:0, one launch (start us, length us, event | category | flops | bytes accessed | tf_op | source)
XLA Modules:
  0.0 1110.7 jit_solution(17548782149290452893)
XLA Ops:
  7.2 16.3 %copy.40 = f32[128,4,64,64]{3,2,1,0:T(8,128)} copy(f32[128,4,64,64]{0,3,2,1:T(8,128)} %param.9) | data formatting | bytes 16777216 | tf_op args[0]
  23.5 23.2 %broadcast_multiply_fusion = f32[128,3,4,64,64]{4,3,2,1,0:T(8,128)} fusion(f32[3,4,64,64]{3,2,1,0:T(8,128)S(1)} %copy-done, f32[128,4,64,64]{3,2,1,0:T(8,128)} %copy.40), kind=kLoop, calls=%fused_computation.5 | loop fusion | flops 6291456 | bytes 33751040 | tf_op jit(solution)/shard_map/mul | solution.py:22
  46.7 40.4 %copy.42 = f32[384,4,64,64]{0,3,2,1:T(8,128)} copy(f32[384,4,64,64]{3,2,1,0:T(8,128)} %bitcast.45) | data formatting | bytes 50331648 | tf_op jit(solution)/shard_map/mul | solution.py:22
  87.1 29.5 %negate_bitcast_fusion = f32[64,64,4,384]{3,1,0,2:T(8,128)} fusion(f32[384,4,64,64]{0,3,2,1:T(8,128)} %copy.42), kind=kOutput, calls=%fused_computation.4 | convolution fusion | flops 4838187008 | bytes 50331648 | tf_op jit(solution)/shard_map/pxyz,zk->ykxp/dot_general | solution.py:25
  116.6 29.9 %convolution_bitcast_fusion = f32[64,64,4,384]{3,1,0,2:T(8,128)} fusion(f32[384,4,64,64]{0,3,2,1:T(8,128)} %copy.42), kind=kOutput, calls=%fused_computation.19 | convolution fusion | flops 4831895552 | bytes 50331648 | tf_op jit(solution)/shard_map/pxyz,zk->ykxp/dot_general | solution.py:24
  146.6 52.3 %fusion.2 = f32[64,64,4,384]{3,0,2,1:T(8,128)} fusion(f32[64,64,4,384]{3,1,0,2:T(8,128)} %negate_bitcast_fusion), kind=kOutput, calls=%fused_computation.8 | convolution fusion | flops 4831895552 | bytes 50331648 | tf_op jit(solution)/shard_map/ly,ykxp->lkxp/dot_general | solution.py:27
  198.9 51.7 %fusion = f32[64,64,4,384]{3,0,2,1:T(8,128)} fusion(f32[64,64,4,384]{3,1,0,2:T(8,128)} %negate_bitcast_fusion), kind=kOutput, calls=%fused_computation.6 | convolution fusion | flops 4831895552 | bytes 50331648 | tf_op jit(solution)/shard_map/ly,ykxp->lkxp/dot_general | solution.py:30
  250.7 54.9 %fusion.10 = f32[64,64,4,384]{3,0,2,1:T(8,128)} fusion(f32[64,64,4,384]{3,0,2,1:T(8,128)} %fusion.2, f32[64,64,4,384]{3,1,0,2:T(8,128)} %convolution_bitcast_fusion), kind=kOutput, calls=%fused_computation.20 | convolution fusion | flops 4838187008 | bytes 75497472 | tf_op jit(solution)/shard_map/ly,ykxp->lkxp/dot_general | solution.py:27
  305.7 21.8 %copy.47 = f32[64,64,4,384]{3,1,0,2:T(8,128)S(1)} copy(f32[64,64,4,384]{3,0,2,1:T(8,128)} %fusion.10) | data formatting | bytes 50331648 | tf_op jit(solution)/shard_map/add | solution.py:27
  327.5 59.9 %copy.48 = f32[4096,4,384]{2,1,0:T(4,128)} copy(f32[4096,4,384]{2,0,1:T(8,128)S(1)} %bitcast.46) | data formatting | bytes 50331648 | tf_op jit(solution)/shard_map/reshape | solution.py:35
  387.3 54.7 %fusion.13 = f32[64,64,4,384]{3,0,2,1:T(8,128)} fusion(f32[64,64,4,384]{3,0,2,1:T(8,128)} %fusion, f32[64,64,4,384]{3,1,0,2:T(8,128)} %convolution_bitcast_fusion), kind=kOutput, calls=%fused_computation.21 | convolution fusion | flops 4838187008 | bytes 75497472 | tf_op jit(solution)/shard_map/ly,ykxp->lkxp/dot_general | solution.py:30
  442.0 21.8 %copy.52 = f32[64,64,4,384]{3,1,0,2:T(8,128)S(1)} copy(f32[64,64,4,384]{3,0,2,1:T(8,128)} %fusion.13) | data formatting | bytes 50331648 | tf_op jit(solution)/shard_map/sub | solution.py:30
  463.8 59.8 %copy.53 = f32[4096,4,384]{2,1,0:T(4,128)} copy(f32[4096,4,384]{2,0,1:T(8,128)S(1)} %bitcast.47) | data formatting | bytes 50331648 | tf_op jit(solution)/shard_map/reshape | solution.py:36
  523.7 53.5 %gather_fusion = f32[4096,4,384]{2,1,0:T(4,128)} fusion(f32[4096,4,384]{2,1,0:T(4,128)} %copy.48, s32[4096]{0:T(1024)S(1)} %get-tuple-element.16), kind=kCustom, calls=%fused_computation.clone | custom fusion | bytes 50348032 | tf_op jit(solution)/shard_map/jit(_take)/gather | solution.py:35
  577.2 53.5 %gather_fusion.1 = f32[4096,4,384]{2,1,0:T(4,128)} fusion(f32[4096,4,384]{2,1,0:T(4,128)} %copy.53, s32[4096]{0:T(1024)S(1)} %get-tuple-element.16), kind=kCustom, calls=%fused_computation.1.clone | custom fusion | bytes 50348032 | tf_op jit(solution)/shard_map/jit(_take)/gather | solution.py:36
  630.7 0.6 fusion.33
  631.3 0.6 copy.49
  631.9 2.0 copy.54
  633.9 82.4 %add_reduce_fusion = (f32[4096,384]{1,0:T(8,128)}, f32[4096,384]{1,0:T(8,128)}) fusion(f32[4096,4,384]{2,1,0:T(4,128)} %gather_fusion.1, f32[4096,4,384]{2,1,0:T(4,128)} %gather_fusion, f32[4096,4]{1,0:T(8,128)} %copy.54, f32[4096,4]{1,0:T(8,128)S(1)} %copy.49, pred[4096]{0:T(1024)(128)(4,1)S(1)} %compare_and_fusion), kind=kLoop, calls=%fused_computation.3 | loop fusion | flops 59768832 | bytes 63049728 | tf_op jit(solution)/shard_map/reduce_sum | solution.py:51
  716.4 10.3 maximum_multiply_fusion
  726.8 137.7 %reduce-scatter.2.cloned.1.call-done = f32[256,768]{1,0:T(8,128)} async-done(((f32[4096,768]{1,0:T(8,128)}), f32[256,768]{1,0:T(8,128)}) %reduce-scatter.2.cloned.1.call-update) | async-done | bytes 786448 | tf_op jit(solution)/shard_map/reduce_scatter | solution.py:68
  864.6 0.1 mul.224
  864.6 0.2 mul.225
  864.9 0.2 sub.40
  865.2 0.2 sub.42
  865.4 0.1 divide_multiply_fusion
  865.5 1.2 fusion.72
  866.7 0.5 broadcast_multiply_fusion.2
  867.2 3.9 maximum_bitcast_fusion
  871.1 95.4 %all-gather.2.cloned.1.call-done = f32[4096,768]{1,0:T(8,128)} async-done(((f32[256,768]{1,0:T(8,128)}), f32[4096,768]{1,0:T(8,128)}) %all-gather.2.cloned.1.call-update) | async-done | bytes 12582928 | tf_op jit(solution)/shard_map/all_gather | solution.py:92
  966.5 108.3 %fusion.8 = f32[2,5,256,4096]{3,2,1,0:T(8,128)} fusion(f32[4096,768]{1,0:T(8,128)} %all-gather.2.cloned.1.call-done, f32[1,5,256,768]{3,2,1,0:T(8,128)} %get-tuple-element.8, f32[1,5,256,768]{3,2,1,0:T(8,128)} %get-tuple-element.7), kind=kOutput, calls=%fused_computation.17 | convolution fusion | flops 96638730240 | bytes 62390272 | tf_op jit(solution)/shard_map/awgk,hk->awgh/dot_general | solution.py:89
  1074.8 28.8 %slice_bitcast_fusion = (f32[5,256,4096]{2,1,0:T(8,128)}, f32[5,256,4096]{2,1,0:T(8,128)}) fusion(f32[2,5,256,4096]{3,2,1,0:T(8,128)} %fusion.8), kind=kLoop, calls=%fused_computation.14 | loop fusion | bytes 83886080 | tf_op jit(solution)/shard_map/squeeze | solution.py:95
  (24 shorter events, 0.3 us)
Async XLA Ops:
  7.2 16.3 %copy-start = (f32[3,4,64,64]{3,2,1,0:T(8,128)S(1)}, f32[3,4,64,64]{3,2,1,0:T(8,128)}, u32[]{:S(2)}) copy-start(f32[3,4,64,64]{3,2,1,0:T(8,128)} %param.10) | copy-start | bytes 589828
  7.2 857.3 %reduce-scatter.2.cloned.1.call-start = ((), (), s32[]{:S(2)}) async-start(), calls=%async_computation.1 | async-start | bytes 13369344 | tf_op jit(solution)/shard_map/reduce_scatter | solution.py:68
  198.9 51.8 %copy-start.1 = (s32[4096]{0:T(1024)S(1)}, s32[4096]{0:T(1024)}, u32[]{:S(2)}) copy-start(s32[4096]{0:T(1024)} %param.15) | copy-start | bytes 49156
  716.3 148.2 %copy-start.4 = (s32[128]{0:T(128)S(1)}, s32[128]{0:T(128)}, u32[]{:S(2)}) copy-start(s32[128]{0:T(128)} %param.13) | copy-start | bytes 1540
  716.3 148.5 %copy-start.2 = (f32[128]{0:T(128)S(1)}, f32[128]{0:T(128)}, u32[]{:S(2)}) copy-start(f32[128]{0:T(128)} %param.11) | copy-start | bytes 1540
  716.4 148.8 %copy-start.3 = (f32[3]{0:T(128)S(1)}, f32[3]{0:T(128)}, u32[]{:S(2)}) copy-start(f32[3]{0:T(128)} %param.12) | copy-start | bytes 40
  716.4 149.0 %copy-start.5 = (f32[5]{0:T(128)S(1)}, f32[5]{0:T(128)}, u32[]{:S(2)}) copy-start(f32[5]{0:T(128)} %param.14) | copy-start | bytes 64
  726.7 239.8 %all-gather.2.cloned.1.call-start = ((), (), s32[]{:S(2)}) async-start(), calls=%async_computation.2 | async-start | bytes 13369344 | tf_op jit(solution)/shard_map/all_gather | solution.py:92
Sparse Core Ops, SparseCore 0:
  726.8 137.6 reduce-scatter.1
  866.8 99.6 all-gather.1
where the time goes:
time: 1120 us; the launch traced here: 1110 us
  matrix products  382 us (34%)
  local copies, waits for them, and re-layouts  360 us (32%)
  waiting for transfers between devices  233 us (21%)
  other arithmetic  121 us (11%)
  between operations  14.4 us (1%)
    reduce_scatter x1, waiting for transfers between devices, body(): lax.psum_scatter(phase_sum(picked, plane_freq, positions, size_x, norm_fa...  138 us
    dot_general x1, matrix products, body(): jnp.einsum('awgk,hk->awgh', left_side, lax.all_gather(owned, 'blk', axis=...  108 us
    all_gather x1, waiting for transfers between devices, body(): lax.all_gather(owned, 'blk', axis=0, tiled=True)  95.4 us
    reduce_sum x1, other arithmetic, phase_sum(): real_m = jnp.sum(real_v * cosine + imag_v * sine, axis=1)  82.4 us
    reshape x1, local copies, waits for them, and re-layouts, plane_picks(): real_b.reshape(size_y * size_z, planes, pair_count)  59.9 us
    reshape x1, local copies, waits for them, and re-layouts, plane_picks(): imag_b.reshape(size_y * size_z, planes, pair_count)  59.8 us
    dot_general x1, matrix products, plane_picks(): jnp.einsum('ly,ykxp->lkxp', cos_y, real_a, precision=highest)  54.9 us
    dot_general x1, matrix products, plane_picks(): jnp.einsum('ly,ykxp->lkxp', sin_y, real_a, precision=highest)  54.7 us
  transfers between devices with their start and end apart: 2, of which 2 were waited for; matrix products, arithmetic and copies ran while one was open for 1% of the time, Pallas kernels for 0%

commit v1 on v0

--- a/solution.py
+++ b/solution.py
@@ -3,6 +3,7 @@
 import jax.numpy as jnp
 from jax import lax
 from jax.sharding import PartitionSpec as P
+from jax.lax import all_to_all, axis_size
 
 highest = lax.Precision.HIGHEST
 
@@ -86,11 +87,17 @@
         [jnp.concatenate([real_w, imag_w], axis=2), jnp.concatenate([imag_w, -real_w], axis=2)],
         axis=0,
     )
+    _choose_matrix = lambda view, comm_axis: jnp.concatenate(
+        all_to_all(
+            jnp.stack(axis_size(comm_axis) * [view], axis=0),
+            axis_name=comm_axis,
+            split_axis=0,
+            concat_axis=0,
+        ),
+        0,
+    )
     chi_both = jnp.einsum(
-        "awgk,hk->awgh",
-        left_side,
-        lax.all_gather(owned, "blk", axis=0, tiled=True),
-        precision=highest,
+        "awgk,hk->awgh", left_side, _choose_matrix(owned, "blk"), precision=highest
     )
     return (chi_both[0], chi_both[1])
 

time: 1120 us -> 1300 us (1.16)
  the two profiles are of different devices: /device:TPU:0 before, /device:TPU:13 now
where the time goes in v1:
time: 1300 us; the launch traced here: 1290 us
  waiting for transfers between devices  402 us (31%)
  matrix products  382 us (29%)
  local copies, waits for them, and re-layouts  366 us (28%)
  other arithmetic  121 us (9%)
  between operations  14.4 us (1%)
    all_to_all x1, waiting for transfers between devices, body(): all_to_all(jnp.stack(axis_size(comm_axis) * [view], axis=0), axis_name=co...  267 us
    reduce_scatter x1, waiting for transfers between devices, body(): lax.psum_scatter(phase_sum(picked, plane_freq, positions, size_x, norm_fa...  135 us
    dot_general x1, matrix products, body(): jnp.einsum('awgk,hk->awgh', left_side, _choose_matrix(owned, 'blk'), prec...  108 us
    reduce_sum x1, other arithmetic, phase_sum(): real_m = jnp.sum(real_v * cosine + imag_v * sine, axis=1)  82.4 us
    reshape x1, local copies, waits for them, and re-layouts, plane_picks(): real_b.reshape(size_y * size_z, planes, pair_count)  59.9 us
    reshape x1, local copies, waits for them, and re-layouts, plane_picks(): imag_b.reshape(size_y * size_z, planes, pair_count)  59.8 us
    dot_general x1, matrix products, plane_picks(): jnp.einsum('ly,ykxp->lkxp', cos_y, real_a, precision=highest)  54.9 us
    dot_general x1, matrix products, plane_picks(): jnp.einsum('ly,ykxp->lkxp', sin_y, real_a, precision=highest)  54.7 us
  transfers between devices with their start and end apart: 2, of which 2 were waited for; matrix products, arithmetic and copies ran while one was open for 0% of the time, Pallas kernels for 0%

profile of v1, /device:TPU:13, one launch (start us, length us, event | category | flops | bytes accessed | tf_op | source)
XLA Modules:
  0.0 1292.0 jit_solution(15202600187276450165)
XLA Ops:
  7.2 16.3 %copy.40 = f32[128,4,64,64]{3,2,1,0:T(8,128)} copy(f32[128,4,64,64]{0,3,2,1:T(8,128)} %param.9) | data formatting | bytes 16777216 | tf_op args[0]
  23.5 23.2 %broadcast_multiply_fusion = f32[128,3,4,64,64]{4,3,2,1,0:T(8,128)} fusion(f32[3,4,64,64]{3,2,1,0:T(8,128)S(1)} %copy-done.1, f32[128,4,64,64]{3,2,1,0:T(8,128)} %copy.40), kind=kLoop, calls=%fused_computation.5 | loop fusion | flops 6291456 | bytes 33751040 | tf_op jit(solution)/shard_map/mul | solution.py:23
  46.7 40.4 %copy.42 = f32[384,4,64,64]{0,3,2,1:T(8,128)} copy(f32[384,4,64,64]{3,2,1,0:T(8,128)} %bitcast.46) | data formatting | bytes 50331648 | tf_op jit(solution)/shard_map/mul | solution.py:23
  87.1 29.5 %negate_bitcast_fusion = f32[64,64,4,384]{3,1,0,2:T(8,128)} fusion(f32[384,4,64,64]{0,3,2,1:T(8,128)} %copy.42), kind=kOutput, calls=%fused_computation.4 | convolution fusion | flops 4838187008 | bytes 50331648 | tf_op jit(solution)/shard_map/pxyz,zk->ykxp/dot_general | solution.py:26
  116.6 29.9 %convolution_bitcast_fusion = f32[64,64,4,384]{3,1,0,2:T(8,128)} fusion(f32[384,4,64,64]{0,3,2,1:T(8,128)} %copy.42), kind=kOutput, calls=%fused_computation.17 | convolution fusion | flops 4831895552 | bytes 50331648 | tf_op jit(solution)/shard_map/pxyz,zk->ykxp/dot_general | solution.py:25
  146.6 52.3 %fusion.2 = f32[64,64,4,384]{3,0,2,1:T(8,128)} fusion(f32[64,64,4,384]{3,1,0,2:T(8,128)} %negate_bitcast_fusion), kind=kOutput, calls=%fused_computation.8 | convolution fusion | flops 4831895552 | bytes 50331648 | tf_op jit(solution)/shard_map/ly,ykxp->lkxp/dot_general | solution.py:28
  198.9 51.7 %fusion = f32[64,64,4,384]{3,0,2,1:T(8,128)} fusion(f32[64,64,4,384]{3,1,0,2:T(8,128)} %negate_bitcast_fusion), kind=kOutput, calls=%fused_computation.6 | convolution fusion | flops 4831895552 | bytes 50331648 | tf_op jit(solution)/shard_map/ly,ykxp->lkxp/dot_general | solution.py:31
  250.7 54.9 %fusion.8 = f32[64,64,4,384]{3,0,2,1:T(8,128)} fusion(f32[64,64,4,384]{3,0,2,1:T(8,128)} %fusion.2, f32[64,64,4,384]{3,1,0,2:T(8,128)} %convolution_bitcast_fusion), kind=kOutput, calls=%fused_computation.18 | convolution fusion | flops 4838187008 | bytes 75497472 | tf_op jit(solution)/shard_map/ly,ykxp->lkxp/dot_general | solution.py:28
  305.7 21.8 %copy.47 = f32[64,64,4,384]{3,1,0,2:T(8,128)S(1)} copy(f32[64,64,4,384]{3,0,2,1:T(8,128)} %fusion.8) | data formatting | bytes 50331648 | tf_op jit(solution)/shard_map/add | solution.py:28
  327.5 59.9 %copy.48 = f32[4096,4,384]{2,1,0:T(4,128)} copy(f32[4096,4,384]{2,0,1:T(8,128)S(1)} %bitcast.47) | data formatting | bytes 50331648 | tf_op jit(solution)/shard_map/reshape | solution.py:36
  387.3 54.7 %fusion.11 = f32[64,64,4,384]{3,0,2,1:T(8,128)} fusion(f32[64,64,4,384]{3,0,2,1:T(8,128)} %fusion, f32[64,64,4,384]{3,1,0,2:T(8,128)} %convolution_bitcast_fusion), kind=kOutput, calls=%fused_computation.19 | convolution fusion | flops 4838187008 | bytes 75497472 | tf_op jit(solution)/shard_map/ly,ykxp->lkxp/dot_general | solution.py:31
  442.0 21.8 %copy.52 = f32[64,64,4,384]{3,1,0,2:T(8,128)S(1)} copy(f32[64,64,4,384]{3,0,2,1:T(8,128)} %fusion.11) | data formatting | bytes 50331648 | tf_op jit(solution)/shard_map/sub | solution.py:31
  463.8 59.8 %copy.53 = f32[4096,4,384]{2,1,0:T(4,128)} copy(f32[4096,4,384]{2,0,1:T(8,128)S(1)} %bitcast.48) | data formatting | bytes 50331648 | tf_op jit(solution)/shard_map/reshape | solution.py:37
  523.7 53.5 %gather_fusion = f32[4096,4,384]{2,1,0:T(4,128)} fusion(f32[4096,4,384]{2,1,0:T(4,128)} %copy.48, s32[4096]{0:T(1024)S(1)} %get-tuple-element.16), kind=kCustom, calls=%fused_computation.clone | custom fusion | bytes 50348032 | tf_op jit(solution)/shard_map/jit(_take)/gather | solution.py:36
  577.2 53.5 %gather_fusion.1 = f32[4096,4,384]{2,1,0:T(4,128)} fusion(f32[4096,4,384]{2,1,0:T(4,128)} %copy.53, s32[4096]{0:T(1024)S(1)} %get-tuple-element.16), kind=kCustom, calls=%fused_computation.1.clone | custom fusion | bytes 50348032 | tf_op jit(solution)/shard_map/jit(_take)/gather | solution.py:37
  630.7 0.6 fusion.32
  631.3 0.6 copy.49
  631.9 2.0 copy.54
  633.9 82.4 %add_reduce_fusion = (f32[4096,384]{1,0:T(8,128)}, f32[4096,384]{1,0:T(8,128)}) fusion(f32[4096,4,384]{2,1,0:T(4,128)} %gather_fusion.1, f32[4096,4,384]{2,1,0:T(4,128)} %gather_fusion, f32[4096,4]{1,0:T(8,128)} %copy.54, f32[4096,4]{1,0:T(8,128)S(1)} %copy.49, pred[4096]{0:T(1024)(128)(4,1)S(1)} %compare_and_fusion), kind=kLoop, calls=%fused_computation.3 | loop fusion | flops 59768832 | bytes 63049728 | tf_op jit(solution)/shard_map/reduce_sum | solution.py:52
  716.3 10.3 maximum_multiply_fusion
  726.7 135.3 %reduce-scatter.2.cloned.1.call-done = f32[256,768]{1,0:T(8,128)} async-done(((f32[4096,768]{1,0:T(8,128)}), f32[256,768]{1,0:T(8,128)}) %reduce-scatter.2.cloned.1.call-update) | async-done | bytes 786448 | tf_op jit(solution)/shard_map/reduce_scatter | solution.py:69
  862.0 7.2 stack.11
  869.1 6.4 all-to-all-start
  875.7 0.2 mul.225
  876.0 0.2 sub.40
  876.2 0.2 sub.42
  876.4 0.1 divide_multiply_fusion
  876.6 0.5 broadcast_multiply_fusion.2
  877.1 3.9 maximum_bitcast_fusion
  881.0 266.8 %all-to-all-done = f32[16,256,768]{2,1,0:T(8,128)} async-done(((f32[16,256,768]{2,1,0:T(8,128)}), f32[16,256,768]{2,1,0:T(8,128)}, u32[]{:S(2)}, u32[]{:S(2)}) %all-to-all-start) | async-done | bytes 12582944 | tf_op jit(solution)/shard_map/all_to_all | solution.py:91
  1147.8 108.3 %fusion.14 = f32[2,5,256,4096]{3,2,1,0:T(8,128)} fusion(f32[4096,768,1,1]{1,0,3,2:T(8,128)} %bitcast.17, f32[1,5,256,768]{3,2,1,0:T(8,128)} %get-tuple-element.8, f32[1,5,256,768]{3,2,1,0:T(8,128)} %get-tuple-element.7), kind=kOutput, calls=%fused_computation.20 | convolution fusion | flops 96638730240 | bytes 62390272 | tf_op jit(solution)/shard_map/awgk,hk->awgh/dot_general | solution.py:99
  1256.1 28.8 %slice_bitcast_fusion = (f32[5,256,4096]{2,1,0:T(8,128)}, f32[5,256,4096]{2,1,0:T(8,128)}) fusion(f32[2,5,256,4096]{3,2,1,0:T(8,128)} %fusion.14), kind=kLoop, calls=%fused_computation.14 | loop fusion | bytes 83886080 | tf_op jit(solution)/shard_map/squeeze | solution.py:102
  (26 shorter events, 0.3 us)
Async XLA Ops:
  7.2 16.3 %copy-start.1 = (f32[3,4,64,64]{3,2,1,0:T(8,128)S(1)}, f32[3,4,64,64]{3,2,1,0:T(8,128)}, u32[]{:S(2)}) copy-start(f32[3,4,64,64]{3,2,1,0:T(8,128)} %param.10) | copy-start | bytes 589828
  7.2 854.8 %reduce-scatter.2.cloned.1.call-start = ((), (), s32[]{:S(2)}) async-start(), calls=%async_computation.2 | async-start | bytes 13369344 | tf_op jit(solution)/shard_map/reduce_scatter | solution.py:69
  198.9 51.8 %copy-start.2 = (s32[4096]{0:T(1024)S(1)}, s32[4096]{0:T(1024)}, u32[]{:S(2)}) copy-start(s32[4096]{0:T(1024)} %param.15) | copy-start | bytes 49156
  726.6 148.9 %copy-start.5 = (s32[128]{0:T(128)S(1)}, s32[128]{0:T(128)}, u32[]{:S(2)}) copy-start(s32[128]{0:T(128)} %param.13) | copy-start | bytes 1540
  726.6 149.2 %copy-start.3 = (f32[128]{0:T(128)S(1)}, f32[128]{0:T(128)}, u32[]{:S(2)}) copy-start(f32[128]{0:T(128)} %param.11) | copy-start | bytes 1540
  726.6 149.5 %copy-start.4 = (f32[3]{0:T(128)S(1)}, f32[3]{0:T(128)}, u32[]{:S(2)}) copy-start(f32[3]{0:T(128)} %param.12) | copy-start | bytes 40
  726.6 149.8 %copy-start.6 = (f32[5]{0:T(128)S(1)}, f32[5]{0:T(128)}, u32[]{:S(2)}) copy-start(f32[5]{0:T(128)} %param.14) | copy-start | bytes 64
  861.9 14.6 %copy-start = (f32[256,768]{1,0:T(8,128)S(1)}, f32[256,768]{1,0:T(8,128)}, u32[]{:S(2)}) copy-start(f32[256,768]{1,0:T(8,128)} %reduce-scatter.2.cloned.1.call-done) | copy-start | bytes 2359300
  869.1 278.7 %all-to-all-start = ((f32[16,256,768]{2,1,0:T(8,128)}), f32[16,256,768]{2,1,0:T(8,128)}, u32[]{:S(2)}, u32[]{:S(2)}) async-start(f32[16,256,768]{2,1,0:T(8,128)} %stack.11), calls=%async_computation.1 | async-start | bytes 25165824 | tf_op jit(solution)/shard_map/all_to_all | solution.py:91
Sparse Core Ops, SparseCore 0:
  726.8 135.1 reduce-scatter.1
